TPU v7x, 32 devices: a whole 2x2x4 slice. The times are simulated.
32 devices in a mesh: dp: 8 (over y, x, core), mp: 4 (over z).
Axes of the slice: x: 2, y: 2, z: 4, core: 2. Of those that a mesh axis runs over, the one named last changes fastest.
Arguments:
- frames_long: bfloat16 [8, 1024, 768], P('dp', 'mp'), may hold values from -6 to 6
- frames_short: bfloat16 [16, 512, 768], P('dp', 'mp'), may hold values from -6 to 6
- length_long: int32 [8], P('dp'), may hold values from 513 to 1024, as said below
- length_short: int32 [16], P('dp'), may hold values from 257 to 512, as said below
- input_proj: bfloat16 [3, 768, 768], P(None, 'dp', 'mp'), may hold values from -0.21875 to 0.21875
- output_proj: bfloat16 [768, 768], P('mp', 'dp'), may hold values from -0.875 to 0.875
- expand_weight: bfloat16 [768, 3072], P('dp', 'mp'), may hold values from -0.21875 to 0.21875
- shrink_weight: bfloat16 [3072, 768], P('mp', 'dp'), may hold values from -0.109375 to 0.109375
- head_bias: bfloat16 [2, 4, 192], P(None, 'mp', 'dp'), may hold values from -3 to 3
- expand_bias: bfloat16 [4, 768], P('mp', 'dp'), may hold values from -3 to 3
- row_params: float32 [6, 768], P(None, ('dp', 'mp')), may hold values from 0.25 to 1.75
- cotangent_long: bfloat16 [8, 1024, 768], P('dp', 'mp'), may hold values from -6 to 6
- cotangent_short: bfloat16 [16, 512, 768], P('dp', 'mp'), may hold values from -6 to 6
Outputs:
- result_long: bfloat16 [8, 1024, 768], P('dp', 'mp')
- result_short: bfloat16 [16, 512, 768], P('dp', 'mp')
- frames_grad_long: float32 [8, 1024, 768], P('dp', 'mp')
- frames_grad_short: float32 [16, 512, 768], P('dp', 'mp')
- input_proj_grad: float32 [3, 768, 768], P(None, 'dp', 'mp')
- output_proj_grad: float32 [768, 768], P('mp', 'dp')
- expand_grad: float32 [768, 3072], P('dp', 'mp')
- shrink_grad: float32 [3072, 768], P('mp', 'dp')
- head_bias_grad: float32 [2, 4, 192], P(None, 'mp', 'dp')
- expand_bias_grad: float32 [4, 768], P('mp', 'dp')
- row_params_grad: float32 [6, 768], P(None, ('dp', 'mp'))
Inputs may be any that keep to these rules, and one draw needn't show every extreme that they name: `length_long`: lengths of the long bucket; some clip has exactly 1024. `length_short`: lengths of the short bucket; some clip has exactly 512.
All inputs are finite; a program needn't handle non-finite values.
Results may differ from a plain program's by a relative error of at most 0.02.
Values may be sent and summed in bfloat16 or wider, within the bound.
No kernel may reach another device: no remote copies, remote signals or barrier semaphores. Data moves between devices by JAX's collectives and lax.ppermute only.
A program may use at most 128 MiB of HBM per device.

v0:
```python
import jax
import jax.numpy as jnp
from jax import lax
from jax.sharding import PartitionSpec as P

HEAD = 64


EPS = 1e-05
QUERY_BLOCK = 512
NEG_FILL = -1e30
CONTRACT_ROWS = (((0,), (0,)), ((), ()))
CONTRACT_COLS = (((1,), (1,)), ((), ()))


def gelu_exact(values):
    return jax.nn.gelu(values, approximate=False)


def flatten_pair(pair):
    return jnp.concatenate([member.reshape(-1, member.shape[-1]) for member in pair], axis=0)


def split_pair(flat_rows, shapes, tail_dims):
    pieces = []
    offset = 0
    for row_count, seq_len in shapes:
        count_here = row_count * seq_len
        pieces.append(
            flat_rows[offset : offset + count_here].reshape((row_count, seq_len) + tail_dims)
        )
        offset = offset + count_here
    return tuple(pieces)


def pair_sum(pair):
    return jnp.sum(pair[0], axis=(0, 1)) + jnp.sum(pair[1], axis=(0, 1))


def norm_rows(values, gain_row, shift_row):
    center = values - jnp.mean(values, axis=-1, keepdims=True)
    inv_dev = lax.rsqrt(jnp.mean(center * center, axis=-1, keepdims=True) + EPS)
    normed = center * inv_dev
    return (normed * gain_row + shift_row, normed, inv_dev)


def norm_back(grad_out, normed, inv_dev, gain_row):
    scaled = grad_out * gain_row
    inner_part = (
        scaled
        - jnp.mean(scaled, axis=-1, keepdims=True)
        - normed * jnp.mean(scaled * normed, axis=-1, keepdims=True)
    )
    return inner_part * inv_dev


def block_scores(q_block, key_rows, lengths):
    seq_len = key_rows.shape[1]
    scores = jnp.einsum(
        "rqhd,rkhd->rhqk", q_block, key_rows, preferred_element_type=jnp.float32
    ) * HEAD ** (-0.5)
    counted = (jnp.arange(seq_len)[None, :] < lengths[:, None])[:, None, None, :]
    return (scores, counted)


def attend(queries, key_rows, value_rows, lengths):
    seq_len = queries.shape[1]
    block_len = min(seq_len, QUERY_BLOCK)
    mixed_list = []
    log_list = []
    for start_at in range(0, seq_len, block_len):
        scores, counted = block_scores(
            queries[:, start_at : start_at + block_len], key_rows, lengths
        )
        scores = jnp.where(counted, scores, NEG_FILL)
        row_max = jnp.max(scores, axis=-1, keepdims=True)
        raised = jnp.exp(scores - row_max)
        totals = jnp.sum(raised, axis=-1, keepdims=True)
        soft_low = (raised / totals).astype(jnp.bfloat16)
        mixed_list.append(
            jnp.einsum("rhqk,rkhd->rqhd", soft_low, value_rows, preferred_element_type=jnp.float32)
        )
        log_list.append(row_max[..., 0] + jnp.log(totals[..., 0]))
    return (jnp.concatenate(mixed_list, axis=1), jnp.concatenate(log_list, axis=2))


def attend_back(queries, key_rows, value_rows, lengths, log_totals, grad_mixed):
    seq_len = queries.shape[1]
    block_len = min(seq_len, QUERY_BLOCK)
    score_scale = HEAD ** (-0.5)
    grad_keys = jnp.zeros(key_rows.shape, jnp.float32)
    grad_values = jnp.zeros(value_rows.shape, jnp.float32)
    grad_query_list = []
    for start_at in range(0, seq_len, block_len):
        q_block = queries[:, start_at : start_at + block_len]
        g_block = grad_mixed[:, start_at : start_at + block_len]
        scores, counted = block_scores(q_block, key_rows, lengths)
        soft_rows = jnp.where(
            counted, jnp.exp(scores - log_totals[:, :, start_at : start_at + block_len, None]), 0.0
        )
        grad_soft = jnp.einsum(
            "rqhd,rkhd->rhqk", g_block, value_rows, preferred_element_type=jnp.float32
        )
        inner_part = jnp.sum(soft_rows * grad_soft, axis=-1, keepdims=True)
        grad_scores = (soft_rows * (grad_soft - inner_part)).astype(jnp.bfloat16)
        grad_query_list.append(
            jnp.einsum("rhqk,rkhd->rqhd", grad_scores, key_rows, preferred_element_type=jnp.float32)
            * score_scale
        )
        grad_keys = (
            grad_keys
            + jnp.einsum(
                "rhqk,rqhd->rkhd", grad_scores, q_block, preferred_element_type=jnp.float32
            )
            * score_scale
        )
        grad_values = grad_values + jnp.einsum(
            "rhqk,rqhd->rkhd",
            soft_rows.astype(jnp.bfloat16),
            g_block,
            preferred_element_type=jnp.float32,
        )
    return (jnp.concatenate(grad_query_list, axis=1), grad_keys, grad_values)


def forward(frames_pair, lengths, weights, row_vals, joined):
    output_w = weights[1]
    expand_w = weights[2]
    shrink_w = weights[3]
    head_b = weights[4]
    expand_b = weights[5]
    frames_all = (
        lax.all_gather(frames_pair[0], "mp", axis=1, tiled=True),
        lax.all_gather(frames_pair[1], "mp", axis=1, tiled=True),
    )
    shapes = tuple(((member.shape[0], member.shape[1]) for member in frames_all))
    flat_in = flatten_pair(frames_all)
    local_width = output_w.shape[0]
    heads_shape = (local_width // HEAD, HEAD)
    project = jnp.dot(flat_in, joined, preferred_element_type=jnp.float32)
    queries = (project[:, :local_width] + head_b[0, 0].astype(jnp.float32)).astype(jnp.bfloat16)
    key_rows = project[:, local_width : 2 * local_width].astype(jnp.bfloat16)
    value_rows = (project[:, 2 * local_width :] + head_b[1, 0].astype(jnp.float32)).astype(
        jnp.bfloat16
    )
    query_pair = split_pair(queries, shapes, heads_shape)
    key_pair = split_pair(key_rows, shapes, heads_shape)
    value_pair = split_pair(value_rows, shapes, heads_shape)
    mixed_list = []
    log_list = []
    for bucket in range(2):
        mixed_rows, log_totals = attend(
            query_pair[bucket], key_pair[bucket], value_pair[bucket], lengths[bucket]
        )
        mixed_list.append(mixed_rows.reshape(-1, local_width))
        log_list.append(log_totals)
    mixed_low = jnp.concatenate(mixed_list, axis=0).astype(jnp.bfloat16)
    attn_parts = split_pair(
        jnp.dot(mixed_low, output_w, preferred_element_type=jnp.float32),
        shapes,
        (output_w.shape[1],),
    )
    attention = (
        lax.psum_scatter(
            attn_parts[0].astype(jnp.bfloat16), "mp", scatter_dimension=1, tiled=True
        ).astype(jnp.float32),
        lax.psum_scatter(
            attn_parts[1].astype(jnp.bfloat16), "mp", scatter_dimension=1, tiled=True
        ).astype(jnp.float32),
    )
    normed_h = []
    normed_one = []
    inv_one = []
    for bucket in range(2):
        value_h, normed, inv_dev = norm_rows(
            frames_pair[bucket].astype(jnp.float32) + attention[bucket] + row_vals[0],
            row_vals[1],
            row_vals[2],
        )
        normed_h.append(value_h)
        normed_one.append(normed)
        inv_one.append(inv_dev)
    h_low = (normed_h[0].astype(jnp.bfloat16), normed_h[1].astype(jnp.bfloat16))
    h_all = (
        lax.all_gather(h_low[0], "mp", axis=1, tiled=True),
        lax.all_gather(h_low[1], "mp", axis=1, tiled=True),
    )
    h_flat = flatten_pair(h_all)
    up_pre = jnp.dot(h_flat, expand_w, preferred_element_type=jnp.float32) + expand_b[0].astype(
        jnp.float32
    )
    activated = gelu_exact(up_pre).astype(jnp.bfloat16)
    feed_parts = split_pair(
        jnp.dot(activated, shrink_w, preferred_element_type=jnp.float32),
        shapes,
        (shrink_w.shape[1],),
    )
    feed_out = (
        lax.psum_scatter(
            feed_parts[0].astype(jnp.bfloat16), "mp", scatter_dimension=1, tiled=True
        ).astype(jnp.float32),
        lax.psum_scatter(
            feed_parts[1].astype(jnp.bfloat16), "mp", scatter_dimension=1, tiled=True
        ).astype(jnp.float32),
    )
    results = []
    normed_two = []
    inv_two = []
    for bucket in range(2):
        value_y, normed, inv_dev = norm_rows(
            normed_h[bucket] + feed_out[bucket] + row_vals[3], row_vals[4], row_vals[5]
        )
        results.append(value_y.astype(jnp.bfloat16))
        normed_two.append(normed)
        inv_two.append(inv_dev)
    kept_values = (
        flat_in,
        query_pair,
        key_pair,
        value_pair,
        tuple(log_list),
        mixed_low,
        tuple(normed_one),
        tuple(inv_one),
        tuple(normed_h),
        h_flat,
        up_pre,
        activated,
        tuple(normed_two),
        tuple(inv_two),
        shapes,
    )
    return (tuple(results), kept_values)


def on_device(
    frames_long,
    frames_short,
    length_long,
    length_short,
    input_proj,
    output_proj,
    expand_weight,
    shrink_weight,
    head_bias,
    expand_bias,
    row_params,
    cotangent_long,
    cotangent_short,
):
    weights = (
        lax.all_gather(input_proj, "dp", axis=1, tiled=True),
        lax.all_gather(output_proj, "dp", axis=1, tiled=True),
        lax.all_gather(expand_weight, "dp", axis=0, tiled=True),
        lax.all_gather(shrink_weight, "dp", axis=1, tiled=True),
        lax.all_gather(head_bias, "dp", axis=2, tiled=True),
        lax.all_gather(expand_bias, "dp", axis=1, tiled=True),
    )
    row_vals = lax.all_gather(row_params, ("dp", "mp"), axis=1, tiled=True)
    input_w = weights[0]
    width_model = input_w.shape[1]
    local_width = input_w.shape[2]
    joined = jnp.transpose(input_w, (1, 0, 2)).reshape(width_model, 3 * local_width)
    lengths = (length_long, length_short)
    results, kept_values = forward((frames_long, frames_short), lengths, weights, row_vals, joined)
    fenced = lax.optimization_barrier(
        (frames_long, frames_short, cotangent_long, cotangent_short, results[0], results[1])
    )
    kept_values = forward((fenced[0], fenced[1]), lengths, weights, row_vals, joined)[1]
    grad_long = fenced[2]
    grad_short = fenced[3]
    (
        flat_in,
        query_pair,
        key_pair,
        value_pair,
        log_pair,
        mixed_low,
        normed_one,
        inv_one,
        normed_h,
        h_flat,
        up_pre,
        activated,
        normed_two,
        inv_two,
        shapes,
    ) = kept_values
    output_w = weights[1]
    expand_w = weights[2]
    shrink_w = weights[3]
    grad_y = (grad_long.astype(jnp.float32), grad_short.astype(jnp.float32))
    grad_z = tuple(
        (
            norm_back(grad_y[bucket], normed_two[bucket], inv_two[bucket], row_vals[4])
            for bucket in range(2)
        )
    )
    feed_low = (grad_z[0].astype(jnp.bfloat16), grad_z[1].astype(jnp.bfloat16))
    feed_all = (
        lax.all_gather(feed_low[0], "mp", axis=1, tiled=True),
        lax.all_gather(feed_low[1], "mp", axis=1, tiled=True),
    )
    feed_flat = flatten_pair(feed_all)
    grad_act = lax.dot_general(
        feed_flat, shrink_w, CONTRACT_COLS, preferred_element_type=jnp.float32
    )
    gelu_back = jax.vjp(gelu_exact, up_pre)[1]
    grad_up = gelu_back(grad_act)[0].astype(jnp.bfloat16)
    grad_shrink = lax.dot_general(
        activated, feed_flat, CONTRACT_ROWS, preferred_element_type=jnp.float32
    )
    grad_expand = lax.dot_general(
        h_flat, grad_up, CONTRACT_ROWS, preferred_element_type=jnp.float32
    )
    grad_expand_bias = jnp.sum(grad_up.astype(jnp.float32), axis=0)[None, :]
    back_parts = split_pair(
        lax.dot_general(grad_up, expand_w, CONTRACT_COLS, preferred_element_type=jnp.float32),
        shapes,
        (width_model,),
    )
    back_h = (
        lax.psum_scatter(
            back_parts[0].astype(jnp.bfloat16), "mp", scatter_dimension=1, tiled=True
        ).astype(jnp.float32),
        lax.psum_scatter(
            back_parts[1].astype(jnp.bfloat16), "mp", scatter_dimension=1, tiled=True
        ).astype(jnp.float32),
    )
    grad_h = tuple((grad_z[bucket] + back_h[bucket] for bucket in range(2)))
    grad_pre = tuple(
        (
            norm_back(grad_h[bucket], normed_one[bucket], inv_one[bucket], row_vals[1])
            for bucket in range(2)
        )
    )
    attn_low = (grad_pre[0].astype(jnp.bfloat16), grad_pre[1].astype(jnp.bfloat16))
    attn_all = (
        lax.all_gather(attn_low[0], "mp", axis=1, tiled=True),
        lax.all_gather(attn_low[1], "mp", axis=1, tiled=True),
    )
    attn_flat = flatten_pair(attn_all)
    grad_mixed = lax.dot_general(
        attn_flat, output_w, CONTRACT_COLS, preferred_element_type=jnp.float32
    ).astype(jnp.bfloat16)
    grad_output = lax.dot_general(
        mixed_low, attn_flat, CONTRACT_ROWS, preferred_element_type=jnp.float32
    )
    mixed_pair = split_pair(grad_mixed, shapes, (local_width // HEAD, HEAD))
    query_list = []
    key_list = []
    value_list = []
    for bucket in range(2):
        grad_q, grad_k, grad_v = attend_back(
            query_pair[bucket],
            key_pair[bucket],
            value_pair[bucket],
            lengths[bucket],
            log_pair[bucket],
            mixed_pair[bucket],
        )
        query_list.append(grad_q.reshape(-1, local_width))
        key_list.append(grad_k.reshape(-1, local_width))
        value_list.append(grad_v.reshape(-1, local_width))
    grad_three = jnp.concatenate(
        [
            jnp.concatenate(query_list, axis=0),
            jnp.concatenate(key_list, axis=0),
            jnp.concatenate(value_list, axis=0),
        ],
        axis=1,
    ).astype(jnp.bfloat16)
    grad_joined = lax.dot_general(
        flat_in, grad_three, CONTRACT_ROWS, preferred_element_type=jnp.float32
    )
    grad_input = jnp.transpose(grad_joined.reshape(width_model, 3, local_width), (1, 0, 2))
    bias_sums = jnp.sum(grad_three.astype(jnp.float32), axis=0)
    grad_head_bias = jnp.stack([bias_sums[:local_width], bias_sums[2 * local_width :]])[:, None, :]
    back_parts_x = split_pair(
        lax.dot_general(grad_three, joined, CONTRACT_COLS, preferred_element_type=jnp.float32),
        shapes,
        (width_model,),
    )
    back_x = (
        lax.psum_scatter(
            back_parts_x[0].astype(jnp.bfloat16), "mp", scatter_dimension=1, tiled=True
        ).astype(jnp.float32),
        lax.psum_scatter(
            back_parts_x[1].astype(jnp.bfloat16), "mp", scatter_dimension=1, tiled=True
        ).astype(jnp.float32),
    )
    frames_grad = tuple((grad_pre[bucket] + back_x[bucket] for bucket in range(2)))
    row_terms = jnp.stack(
        [
            pair_sum(grad_pre),
            pair_sum((grad_h[0] * normed_one[0], grad_h[1] * normed_one[1])),
            pair_sum(grad_h),
            pair_sum(grad_z),
            pair_sum((grad_y[0] * normed_two[0], grad_y[1] * normed_two[1])),
            pair_sum(grad_y),
        ]
    )
    row_grads = lax.psum_scatter(row_terms, ("dp", "mp"), scatter_dimension=1, tiled=True)
    shares = (
        lax.psum_scatter(grad_input, "dp", scatter_dimension=1, tiled=True),
        lax.psum_scatter(grad_output, "dp", scatter_dimension=1, tiled=True),
        lax.psum_scatter(grad_expand, "dp", scatter_dimension=0, tiled=True),
        lax.psum_scatter(grad_shrink, "dp", scatter_dimension=1, tiled=True),
        lax.psum_scatter(grad_head_bias, "dp", scatter_dimension=2, tiled=True),
        lax.psum_scatter(grad_expand_bias, "dp", scatter_dimension=1, tiled=True),
    )
    return (
        results[0],
        results[1],
        frames_grad[0],
        frames_grad[1],
        shares[0],
        shares[1],
        shares[2],
        shares[3],
        shares[4],
        shares[5],
        row_grads,
    )


def solution(mesh):
    return jax.shard_map(
        on_device,
        mesh=mesh,
        in_specs=(
            P("dp", "mp", None),
            P("dp", "mp", None),
            P("dp"),
            P("dp"),
            P(None, "dp", "mp"),
            P("mp", "dp"),
            P("dp", "mp"),
            P("mp", "dp"),
            P(None, "mp", "dp"),
            P("mp", "dp"),
            P(None, ("dp", "mp")),
            P("dp", "mp", None),
            P("dp", "mp", None),
        ),
        out_specs=(
            P("dp", "mp", None),
            P("dp", "mp", None),
            P("dp", "mp", None),
            P("dp", "mp", None),
            P(None, "dp", "mp"),
            P("mp", "dp"),
            P("dp", "mp"),
            P("mp", "dp"),
            P(None, "mp", "dp"),
            P("mp", "dp"),
            P(None, ("dp", "mp")),
        ),
        check_vma=False,
    )
```

profile of v0, /device:TPU:0, one launch (start us, length us, event | category | flops | bytes accessed | tf_op | source)
XLA Modules:
  0.0 1208.1 jit_solution(8948179500124435396)
XLA Ops:
  12.9 14.6 %all_gather.59 = bf16[3,768,192]{2,0,1:T(4,128)(2,1)S(1)} all-gather(bf16[3,96,192]{2,0,1:T(4,128)(2,1)S(1)} %copy.92), channel_id=1, replica_groups=mesh['dp'=8,'mp'=4] {'dp'}, dimensions={1}, use_global_device_ids=true | all-gather | bytes 995328 | tf_op jit(solution)/shard_map/all_gather | solution.py:252
  50.2 37.6 %all-gather.18.cloned.1.call-done = bf16[2,512,768]{2,1,0:T(8,128)(2,1)} async-done(((bf16[2,128,768]{2,1,0:T(8,128)(2,1)}), bf16[2,512,768]{2,1,0:T(8,128)(2,1)}) %all-gather.18.cloned.1.call-update) | async-done | bytes 1572880 | tf_op jit(solution)/shard_map/all_gather | solution.py:134
  121.3 70.6 %all-gather = f32[32,24,6]{1,2,0:T(8,128)S(1)} all-gather(f32[1,24,6]{1,2,0:T(8,128)S(1)} %bitcast.304), channel_id=1, replica_groups=mesh['dp'=8,'mp'=4] {'dp','mp'}, dimensions={0}, use_global_device_ids=true | all-gather | bytes 19008 | tf_op jit(solution)/shard_map/all_gather | solution.py:259
  215.9 14.1 %all-gather.22.cloned.1.call-done = bf16[2,512,768]{2,1,0:T(8,128)(2,1)} async-done(((bf16[2,128,768]{2,1,0:T(8,128)(2,1)}), bf16[2,512,768]{2,1,0:T(8,128)(2,1)}) %all-gather.22.cloned.1.call-update) | async-done | bytes 1572880 | tf_op jit(solution)/shard_map/all_gather | solution.py:186
  230.0 38.0 %all-gather.20.cloned.1.call-done = bf16[1,1024,768]{2,1,0:T(8,128)(2,1)} async-done(((bf16[1,256,768]{2,1,0:T(8,128)(2,1)}), bf16[1,1024,768]{2,1,0:T(8,128)(2,1)}) %all-gather.20.cloned.1.call-update) | async-done | bytes 1572880 | tf_op jit(solution)/shard_map/all_gather | solution.py:185
  267.9 21.2 %convolution_convert_fusion.2 = bf16[2048,768]{1,0:T(8,128)(2,1)} fusion(bf16[768,768]{0,1:T(8,128)(2,1)} %all-gather.26.cloned.1.call-done, bf16[768,768]{1,0:T(8,128)(2,1)} %all-gather.24.cloned.1.call-done, bf16[1024,768]{1,0:T(8,128)(2,1)} %bitcast.323, bf16[1024,768]{1,0:T(8,128)(2,1)} %bitcast.324, f32[768]{0:T(1024)S(1)} %add.496), kind=kOutput, calls=%fused_computation.76 | convolution fusion | flops 4943511552 | bytes 8653824 | tf_op jit(solution)/shard_map/dot_general | solution.py:194
  293.8 33.5 %reduce-scatter.28.cloned.1.call-done = bf16[1,256,768]{2,1,0:T(8,128)(2,1)} async-done(((bf16[1,1024,768]{2,1,0:T(8,128)(2,1)}), bf16[1,256,768]{2,1,0:T(8,128)(2,1)}) %reduce-scatter.28.cloned.1.call-update) | async-done | bytes 393232 | tf_op jit(solution)/shard_map/reduce_scatter | solution.py:199
  329.0 34.9 %reduce-scatter.30.cloned.1.call-done = bf16[2,128,768]{2,1,0:T(8,128)(2,1)} async-done(((bf16[2,512,768]{2,1,0:T(8,128)(2,1)}), bf16[2,128,768]{2,1,0:T(8,128)(2,1)}) %reduce-scatter.30.cloned.1.call-update) | async-done | bytes 393232 | tf_op jit(solution)/shard_map/reduce_scatter | solution.py:202
  370.9 35.3 %all-gather.28.cloned.1.call-done = bf16[1,1024,768]{2,1,0:T(8,128)(2,1)} async-done(((bf16[1,256,768]{2,1,0:T(8,128)(2,1)}), bf16[1,1024,768]{2,1,0:T(8,128)(2,1)}) %all-gather.28.cloned.1.call-update) | async-done | bytes 1572880 | tf_op jit(solution)/shard_map/all_gather | solution.py:133
  406.2 37.4 %all-gather.30.cloned.1.call-done = bf16[2,512,768]{2,1,0:T(8,128)(2,1)} async-done(((bf16[2,128,768]{2,1,0:T(8,128)(2,1)}), bf16[2,512,768]{2,1,0:T(8,128)(2,1)}) %all-gather.30.cloned.1.call-update) | async-done | bytes 1572880 | tf_op jit(solution)/shard_map/all_gather | solution.py:134
  475.8 33.6 %reduce-scatter.34.cloned.1.call-done = bf16[2,128,768]{2,1,0:T(8,128)(2,1)} async-done(((bf16[2,512,768]{2,1,0:T(8,128)(2,1)}), bf16[2,128,768]{2,1,0:T(8,128)(2,1)}) %reduce-scatter.34.cloned.1.call-update) | async-done | bytes 393232 | tf_op jit(solution)/shard_map/reduce_scatter | solution.py:167
  513.9 49.7 %reduce-scatter.32.cloned.1.call-done = bf16[1,256,768]{2,1,0:T(8,128)(2,1)} async-done(((bf16[1,1024,768]{2,1,0:T(8,128)(2,1)}), bf16[1,256,768]{2,1,0:T(8,128)(2,1)}) %reduce-scatter.32.cloned.1.call-update) | async-done | bytes 393232 | tf_op jit(solution)/shard_map/reduce_scatter | solution.py:164
  570.1 38.5 %all-gather.32.cloned.1.call-done = bf16[1,1024,768]{2,1,0:T(8,128)(2,1)} async-done(((bf16[1,256,768]{2,1,0:T(8,128)(2,1)}), bf16[1,1024,768]{2,1,0:T(8,128)(2,1)}) %all-gather.32.cloned.1.call-update) | async-done | bytes 1572880 | tf_op jit(solution)/shard_map/all_gather | solution.py:185
  608.6 19.3 %multiply_convert_fusion.3 = (bf16[2048,768]{1,0:T(8,128)(2,1)S(1)}, f32[2048,768]{1,0:T(8,128)}, f32[2048,768]{1,0:T(8,128)}) fusion(f32[768]{0:T(1024)S(1)} %copy-done.84, bf16[768,768]{1,0:T(8,128)(2,1)S(1)} %copy-done.89, bf16[1024,768]{1,0:T(8,128)(2,1)} %bitcast.311, bf16[1024,768]{1,0:T(8,128)(2,1)} %bitcast.313), kind=kOutput, calls=%fused_computation.20 | convolution fusion | flops 2526019584 | bytes 20057088 | tf_op jit(solution)/shard_map/dot_general | solution.py:189
  633.5 33.7 %reduce-scatter.38.cloned.1.call-done = bf16[2,128,768]{2,1,0:T(8,128)(2,1)} async-done(((bf16[2,512,768]{2,1,0:T(8,128)(2,1)}), bf16[2,128,768]{2,1,0:T(8,128)(2,1)}) %reduce-scatter.38.cloned.1.call-update) | async-done | bytes 393232 | tf_op jit(solution)/shard_map/reduce_scatter | solution.py:202
  670.9 50.6 %reduce-scatter.36.cloned.1.call-done = bf16[1,256,768]{2,1,0:T(8,128)(2,1)} async-done(((bf16[1,1024,768]{2,1,0:T(8,128)(2,1)}), bf16[1,256,768]{2,1,0:T(8,128)(2,1)}) %reduce-scatter.36.cloned.1.call-update) | async-done | bytes 393232 | tf_op jit(solution)/shard_map/reduce_scatter | solution.py:199
  728.0 38.3 %all-gather.36.cloned.1.call-done = bf16[1,1024,768]{2,1,0:T(8,128)(2,1)} async-done(((bf16[1,256,768]{2,1,0:T(8,128)(2,1)}), bf16[1,1024,768]{2,1,0:T(8,128)(2,1)}) %all-gather.36.cloned.1.call-update) | async-done | bytes 1572880 | tf_op jit(solution)/shard_map/all_gather | solution.py:301
  783.0 33.5 %reduce-scatter.42.cloned.1.call-done = bf16[2,128,768]{2,1,0:T(8,128)(2,1)} async-done(((bf16[2,512,768]{2,1,0:T(8,128)(2,1)}), bf16[2,128,768]{2,1,0:T(8,128)(2,1)}) %reduce-scatter.42.cloned.1.call-update) | async-done | bytes 393232 | tf_op jit(solution)/shard_map/reduce_scatter | solution.py:326
  822.3 48.6 %reduce-scatter.40.cloned.1.call-done = bf16[1,256,768]{2,1,0:T(8,128)(2,1)} async-done(((bf16[1,1024,768]{2,1,0:T(8,128)(2,1)}), bf16[1,256,768]{2,1,0:T(8,128)(2,1)}) %reduce-scatter.40.cloned.1.call-update) | async-done | bytes 393232 | tf_op jit(solution)/shard_map/reduce_scatter | solution.py:323
  880.9 34.2 %all-gather.40.cloned.1.call-done = bf16[1,1024,768]{2,1,0:T(8,128)(2,1)} async-done(((bf16[1,256,768]{2,1,0:T(8,128)(2,1)}), bf16[1,1024,768]{2,1,0:T(8,128)(2,1)}) %all-gather.40.cloned.1.call-update) | async-done | bytes 1572880 | tf_op jit(solution)/shard_map/all_gather | solution.py:339
  989.0 42.2 %all-reduce.2 = f32[6,768]{1,0:T(8,128)S(1)} all-reduce(f32[6,768]{1,0:T(8,128)S(1)} %stack.21), channel_id=20, replica_groups=mesh['dp'=8,'mp'=4] {'dp','mp'}, use_global_device_ids=true, to_apply=%region_71.72.clone | all-reduce | flops 4608 | bytes 36864
  1064.0 43.2 %reduce-scatter.50.cloned.1.call-done = f32[96,768]{1,0:T(8,128)} async-done(((f32[768,768]{1,0:T(8,128)}), f32[96,768]{1,0:T(8,128)}) %reduce-scatter.50.cloned.1.call-update) | async-done | bytes 294928 | tf_op jit(solution)/shard_map/reduce_scatter | solution.py:407
  1107.3 46.7 %reduce-scatter.52.cloned.1.call-done = f32[768,96]{0,1:T(8,128)} async-done(((f32[768,768]{0,1:T(8,128)}), f32[768,96]{0,1:T(8,128)}) %reduce-scatter.52.cloned.1.call-update) | async-done | bytes 294928 | tf_op jit(solution)/shard_map/reduce_scatter | solution.py:408
  1154.0 46.1 %reduce-scatter.48.cloned.1.call-done = f32[3,96,192]{2,1,0:T(8,128)} async-done(((f32[3,768,192]{2,1,0:T(8,128)}), f32[3,96,192]{2,1,0:T(8,128)}) %reduce-scatter.48.cloned.1.call-update) | async-done | bytes 221200 | tf_op jit(solution)/shard_map/reduce_scatter | solution.py:405
  (463 shorter events, 292.2 us)
Async XLA Ops:
  9.5 182.7 %reduce-scatter.26.cloned.1.call-start = ((), (), s32[]{:S(2)}) async-start(), calls=%async_computation.21 | async-start | bytes 1966080 | tf_op jit(solution)/shard_map/reduce_scatter | solution.py:167
  120.1 95.8 %all-gather.24.cloned.1.call-start = ((), (), s32[]{:S(2)}) async-start(), calls=%async_computation.23 | async-start | bytes 1327104 | tf_op jit(solution)/shard_map/all_gather | solution.py:254
  120.7 95.2 %all-gather.26.cloned.1.call-start = ((), (), s32[]{:S(2)}) async-start(), calls=%async_computation.24 | async-start | bytes 1327104 | tf_op jit(solution)/shard_map/all_gather | solution.py:255
  121.3 108.7 %all-gather.22.cloned.1.call-start = ((), (), s32[]{:S(2)}) async-start(), calls=%async_computation.22 | async-start | bytes 1966080 | tf_op jit(solution)/shard_map/all_gather | solution.py:186
  201.3 126.0 %reduce-scatter.28.cloned.1.call-start = ((), (), s32[]{:S(2)}) async-start(), calls=%async_computation.25 | async-start | bytes 1966080 | tf_op jit(solution)/shard_map/reduce_scatter | solution.py:199
  293.8 112.4 %all-gather.28.cloned.1.call-start = ((), (), s32[]{:S(2)}) async-start(), calls=%async_computation.27 | async-start | bytes 1966080 | tf_op jit(solution)/shard_map/all_gather | solution.py:133
  370.7 138.7 %reduce-scatter.34.cloned.1.call-start = ((), (), s32[]{:S(2)}) async-start(), calls=%async_computation.31 | async-start | bytes 1966080 | tf_op jit(solution)/shard_map/reduce_scatter | solution.py:167
  475.7 94.4 %all-gather.34.cloned.1.call-start = ((), (), s32[]{:S(2)}) async-start(), calls=%async_computation.32 | async-start | bytes 1966080 | tf_op jit(solution)/shard_map/all_gather | solution.py:186
  513.9 94.7 %all-gather.32.cloned.1.call-start = ((), (), s32[]{:S(2)}) async-start(), calls=%async_computation.30 | async-start | bytes 1966080 | tf_op jit(solution)/shard_map/all_gather | solution.py:185
  568.2 98.9 %reduce-scatter.38.cloned.1.call-start = ((), (), s32[]{:S(2)}) async-start(), calls=%async_computation.35 | async-start | bytes 1966080 | tf_op jit(solution)/shard_map/reduce_scatter | solution.py:202
  632.8 88.7 %reduce-scatter.36.cloned.1.call-start = ((), (), s32[]{:S(2)}) async-start(), calls=%async_computation.33 | async-start | bytes 1966080 | tf_op jit(solution)/shard_map/reduce_scatter | solution.py:199
  633.4 94.6 %all-gather.38.cloned.1.call-start = ((), (), s32[]{:S(2)}) async-start(), calls=%async_computation.36 | async-start | bytes 1966080 | tf_op jit(solution)/shard_map/all_gather | solution.py:302
  670.8 95.5 %all-gather.36.cloned.1.call-start = ((), (), s32[]{:S(2)}) async-start(), calls=%async_computation.34 | async-start | bytes 1966080 | tf_op jit(solution)/shard_map/all_gather | solution.py:301
  726.2 90.3 %reduce-scatter.42.cloned.1.call-start = ((), (), s32[]{:S(2)}) async-start(), calls=%async_computation.39 | async-start | bytes 1966080 | tf_op jit(solution)/shard_map/reduce_scatter | solution.py:326
  782.2 88.7 %reduce-scatter.40.cloned.1.call-start = ((), (), s32[]{:S(2)}) async-start(), calls=%async_computation.37 | async-start | bytes 1966080 | tf_op jit(solution)/shard_map/reduce_scatter | solution.py:323
  782.9 98.0 %all-gather.42.cloned.1.call-start = ((), (), s32[]{:S(2)}) async-start(), calls=%async_computation.40 | async-start | bytes 1966080 | tf_op jit(solution)/shard_map/all_gather | solution.py:340
  822.3 92.8 %all-gather.40.cloned.1.call-start = ((), (), s32[]{:S(2)}) async-start(), calls=%async_computation.38 | async-start | bytes 1966080 | tf_op jit(solution)/shard_map/all_gather | solution.py:339
  876.8 110.7 %reduce-scatter.56.cloned.1.call-start = ((), (), s32[]{:S(2)}) async-start(), calls=%async_computation.47 | async-start | bytes 442368
  880.6 167.2 %reduce-scatter.54.cloned.1.call-start = ((), (), s32[]{:S(2)}) async-start(), calls=%async_computation.46 | async-start | bytes 884736
  953.0 96.5 %reduce-scatter.46.cloned.1.call-start = ((), (), s32[]{:S(2)}) async-start(), calls=%async_computation.42 | async-start | bytes 1966080 | tf_op jit(solution)/shard_map/reduce_scatter | solution.py:388
  965.7 96.4 %reduce-scatter.44.cloned.1.call-start = ((), (), s32[]{:S(2)}) async-start(), calls=%async_computation.41 | async-start | bytes 1966080 | tf_op jit(solution)/shard_map/reduce_scatter | solution.py:385
  966.5 140.8 %reduce-scatter.50.cloned.1.call-start = ((), (), s32[]{:S(2)}) async-start(), calls=%async_computation.44 | async-start | bytes 2654208 | tf_op jit(solution)/shard_map/reduce_scatter | solution.py:407
  973.0 180.9 %reduce-scatter.52.cloned.1.call-start = ((), (), s32[]{:S(2)}) async-start(), calls=%async_computation.45 | async-start | bytes 2654208 | tf_op jit(solution)/shard_map/reduce_scatter | solution.py:408
  980.1 220.0 %reduce-scatter.48.cloned.1.call-start = ((), (), s32[]{:S(2)}) async-start(), calls=%async_computation.43 | async-start | bytes 2654208 | tf_op jit(solution)/shard_map/reduce_scatter | solution.py:405
  (111 other events, 3320.3 us)
Sparse Core Ops, SparseCore 0:
  10.4 39.7 all-gather.15
  51.8 35.9 all-gather.17
  119.6 35.2 reduce-scatter.25
  157.1 35.0 reduce-scatter.23
  370.2 35.9 all-gather.27
  407.6 35.9 all-gather.29
  514.0 56.0 all-gather.33
  572.2 36.3 all-gather.31
  633.0 34.1 reduce-scatter.37
  669.3 52.1 reduce-scatter.35
  822.4 54.8 all-gather.41
  878.7 36.3 all-gather.39
Sparse Core Ops, SparseCore 1:
  122.4 22.8 all-gather.23
  147.1 23.9 all-gather.25
  196.7 33.1 all-gather.21
  232.1 35.8 all-gather.19
  293.1 34.1 reduce-scatter.27
  329.6 34.1 reduce-scatter.29
  475.2 34.1 reduce-scatter.33
  511.6 52.1 reduce-scatter.31
  670.9 57.0 all-gather.37
  730.2 36.1 all-gather.35
  782.2 34.1 reduce-scatter.41
  818.7 52.1 reduce-scatter.39
  880.7 32.2 reduce-scatter.55
  953.0 33.8 reduce-scatter.53
  989.2 36.3 reduce-scatter.45
  1027.9 34.1 reduce-scatter.43
  1066.0 41.2 reduce-scatter.49
  1111.6 42.3 reduce-scatter.51
  1157.7 42.3 reduce-scatter.47
where the time goes:
time: 1220 us; the launch traced here: 1210 us
  waiting for transfers between devices  750 us (61%)
  blocking collectives  171 us (14%)
  matrix products  163 us (13%)
  other arithmetic  65.1 us (5%)
  local copies, waits for them, and re-layouts  35.7 us (3%)
  between operations  20.4 us (2%)
    reduce_scatter x2, waiting for transfers between devices, forward(): lax.psum_scatter(feed_parts[0].astype(jnp.bfloat16), 'mp', scatter_dimens...  84.1 us
    all_gather x2, waiting for transfers between devices, forward(): lax.all_gather(h_low[0], 'mp', axis=1, tiled=True)  76.5 us
    all_gather x2, waiting for transfers between devices, forward(): lax.all_gather(frames_pair[1], 'mp', axis=1, tiled=True)  75 us
    all_gather x1, blocking collectives, on_device(): row_vals = lax.all_gather(row_params, ('dp', 'mp'), axis=1, tiled=True)  70.6 us
    reduce_scatter x2, waiting for transfers between devices, forward(): lax.psum_scatter(feed_parts[1].astype(jnp.bfloat16), 'mp', scatter_dimens...  68.5 us
    unnamed x3, blocking collectives  68.2 us
    reduce_scatter x2, waiting for transfers between devices, forward(): lax.psum_scatter(attn_parts[0].astype(jnp.bfloat16), 'mp', scatter_dimens...  49.8 us
    reduce_scatter x1, waiting for transfers between devices, on_device(): lax.psum_scatter(back_parts[0].astype(jnp.bfloat16), 'mp', scatter_dimens...  48.6 us
  transfers between devices with their start and end apart: 31, of which 23 were waited for; matrix products, arithmetic and copies ran while one was open for 11% of the time, Pallas kernels for 0%

commit v1 on v0

v1 whole, which is shorter than its diff:
```python
import functools

import jax
import jax.numpy as jnp
from jax import lax
from jax.experimental import pallas as pl
from jax.experimental.pallas import tpu as pltpu
from jax.sharding import PartitionSpec as P

HEAD = 64
EPS = 1e-05
NEG_FILL = -1e30
SCALE = HEAD ** (-0.5)
N_MP = 4
LANES = 128
Q_TILE = 256
F32 = jnp.float32
BF16 = jnp.bfloat16
NT = (((1,), (1,)), ((), ()))
NN = (((1,), (0,)), ((), ()))
TN = (((0,), (0,)), ((), ()))


def dot(left, right, dims):
    return lax.dot_general(left, right, dims, preferred_element_type=F32)


def mp_swap(value, step):
    return lax.ppermute(value, "mp", [(i, i ^ step) for i in range(N_MP)])


def dp_swap(value, target):
    size = lax.axis_size("dp")
    return lax.ppermute(value, "dp", [(i, target(i)) for i in range(size)])


def core_swap(value):
    return dp_swap(value, lambda i: i ^ 1)


def to_clips(long_rows, short_rows, core, depth):
    block = short_rows.shape[1]
    keep = lax.dynamic_slice_in_dim(long_rows, core * block, block, 0)
    away = lax.dynamic_slice_in_dim(long_rows, (1 - core) * block, block, 0)
    back = core_swap(away)
    first = jnp.where(core == 0, keep, back)
    second = jnp.where(core == 0, back, keep)
    blocks = jnp.stack([first, second, short_rows[0], short_rows[1]])
    parts = []
    for step in range(N_MP):
        piece = lax.dynamic_index_in_dim(blocks, depth ^ step, 0, keepdims=False)
        parts.append(piece if step == 0 else mp_swap(piece, step))
    return jnp.concatenate(parts, axis=0)


def from_clips(rows, core, depth):
    block = rows.shape[0] // N_MP
    parts = []
    for step in range(N_MP):
        piece = rows[step * block : (step + 1) * block]
        parts.append(piece if step == 0 else mp_swap(piece, step))
    blocks = jnp.stack(parts)
    first, second, short_a, short_b = (
        lax.dynamic_index_in_dim(blocks, depth ^ i, 0, keepdims=False) for i in range(N_MP)
    )
    keep = jnp.where(core == 0, first, second)
    away = jnp.where(core == 0, second, first)
    back = core_swap(away)
    low = jnp.where(core == 0, keep, back)
    high = jnp.where(core == 0, back, keep)
    return jnp.concatenate([low, high], axis=0)[None], jnp.stack([short_a, short_b])


def bit_of(core_index, late):
    even = 4 if late else 2
    return even if core_index == 0 else 6 - even


def slot_table(mine):
    core = mine % 2
    early = jnp.where(core == 0, 2, 4)
    late = 6 - early
    relative = [0, early, late, 6, 1, 1 ^ late, 1 ^ early, 7]
    return jnp.stack([mine ^ r for r in relative]).astype(jnp.int32)


def place_kernel(n_pieces, table, *refs):
    pieces, out, sems = refs[:n_pieces], refs[n_pieces], refs[n_pieces + 1]
    at = 0
    copies = []
    for piece in pieces:
        for k in range(piece.shape[0]):
            copy = pltpu.make_async_copy(piece.at[k], out.at[table[at]], sems.at[at])
            copy.start()
            copies.append(copy)
            at += 1
    for copy in copies:
        copy.wait()


def place(pieces, table):
    total = sum(p.shape[0] for p in pieces)
    _, rows, cols = pieces[0].shape
    out = pl.pallas_call(
        functools.partial(place_kernel, len(pieces)),
        out_shape=jax.ShapeDtypeStruct((total, rows, cols), pieces[0].dtype),
        grid_spec=pltpu.PrefetchScalarGridSpec(
            num_scalar_prefetch=1,
            grid=(1,),
            in_specs=[pl.BlockSpec(memory_space=pl.ANY)] * len(pieces),
            out_specs=pl.BlockSpec(memory_space=pl.ANY),
            scratch_shapes=[pltpu.SemaphoreType.DMA((total,))],
        ),
        name="place",
    )(table, *pieces)
    return out.reshape(total * rows, cols)


def mp_gather(shard):
    return [shard] + [mp_swap(shard, step) for step in range(1, N_MP)]


def dp_gather(slab):
    size = lax.axis_size("dp")
    if size != 8:
        return lax.all_gather(slab, "dp", axis=0, tiled=True)
    own = slab[None]
    one = dp_swap(own, lambda i: i ^ bit_of(i % 2, False))
    two = dp_swap(jnp.concatenate([own, one]), lambda i: i ^ bit_of(i % 2, True))
    rest = core_swap(jnp.concatenate([own, one, two]))
    return place([own, one, two, rest], slot_table(lax.axis_index("dp")))


def dp_scatter(grad):
    size = lax.axis_size("dp")
    if size != 8:
        return lax.psum_scatter(grad, "dp", scatter_dimension=0, tiled=True)
    rows, cols = grad.shape
    table = slot_table(lax.axis_index("dp"))
    slots = grad.reshape(size, rows // size, cols)

    def pick(indices):
        return jnp.stack(
            [lax.dynamic_index_in_dim(slots, table[i], 0, keepdims=False) for i in indices]
        )

    away = pick((4, 5, 6, 7)).astype(BF16)
    keep = pick((0, 1, 2, 3))
    total = keep + core_swap(away).astype(F32)
    away = dp_swap(total[2:].astype(BF16), lambda i: i ^ bit_of(i % 2, True))
    total = total[:2] + away.astype(F32)
    away = dp_swap(total[1].astype(BF16), lambda i: i ^ bit_of(i % 2, False))
    return total[0] + away.astype(F32)


def mp_scatter(parts):
    total = parts[0]
    for step in range(1, N_MP):
        total = total + mp_swap(parts[step].astype(BF16), step).astype(F32)
    return total


def attend_kernel(q_ref, k_ref, v_ref, kp_ref, vp_ref, bias_ref, o_ref, lse_ref):
    rows = q_ref.shape[0]
    keys = jnp.concatenate([k_ref[...], kp_ref[...]], axis=0)
    values = jnp.concatenate([v_ref[...], vp_ref[...]], axis=0)
    bias = bias_ref[...]
    tile = min(rows, Q_TILE)
    low = lax.broadcasted_iota(jnp.int32, (tile, LANES), 1) < HEAD
    for start in range(0, rows, tile):
        q = q_ref[start : start + tile, :]
        outs, logs = [], []
        for half in range(2):
            here = low if half == 0 else ~low
            q_here = jnp.where(here, q, jnp.zeros_like(q))
            scores = dot(q_here, keys, NT) + bias
            top = jnp.max(scores, axis=-1, keepdims=True)
            raised = jnp.exp(scores - top)
            total = jnp.sum(raised, axis=-1, keepdims=True)
            mixed = dot(raised.astype(BF16), values, NN)
            outs.append(mixed / total)
            logs.append(top + jnp.log(total))
        o_ref[start : start + tile, :] = jnp.where(low, outs[0], outs[1]).astype(BF16)
        lse_ref[start : start + tile, :] = jnp.where(low, logs[0], logs[1])


def attend(qkv, kv_other, bias):
    rows, width = qkv.shape[0], qkv.shape[1] // 3
    pairs = width // LANES
    spec = lambda base: pl.BlockSpec((rows, LANES), lambda p: (0, base + p))
    return pl.pallas_call(
        attend_kernel,
        out_shape=(
            jax.ShapeDtypeStruct((rows, width), BF16),
            jax.ShapeDtypeStruct((rows, width), F32),
        ),
        grid=(pairs,),
        in_specs=[
            spec(0),
            spec(pairs),
            spec(2 * pairs),
            spec(0),
            spec(pairs),
            pl.BlockSpec((1, 2 * rows), lambda p: (0, 0)),
        ],
        out_specs=(spec(0), spec(0)),
        compiler_params=pltpu.CompilerParams(vmem_limit_bytes=56 << 20),
        name="attend",
    )(qkv, qkv, qkv, kv_other, kv_other, bias)


def attend_back_kernel(
    q_ref, k_ref, v_ref, kp_ref, vp_ref, bias_ref, o_ref, lse_ref, do_ref,
    dq_ref, dk_ref, dv_ref, dkp_ref, dvp_ref,
):
    rows = q_ref.shape[0]
    keys = jnp.concatenate([k_ref[...], kp_ref[...]], axis=0)
    values = jnp.concatenate([v_ref[...], vp_ref[...]], axis=0)
    bias = bias_ref[...]
    tile = min(rows, Q_TILE)
    low = lax.broadcasted_iota(jnp.int32, (tile, LANES), 1) < HEAD
    dk = jnp.zeros((LANES, 2 * rows), F32)
    dv = jnp.zeros((LANES, 2 * rows), F32)
    for start in range(0, rows, tile):
        at = slice(start, start + tile)
        q, do = q_ref[at, :], do_ref[at, :]
        product = o_ref[at, :].astype(F32) * do.astype(F32)
        lse = lse_ref[at, :]
        outs = []
        for half in range(2):
            here = low if half == 0 else ~low
            q_here = jnp.where(here, q, jnp.zeros_like(q))
            do_here = jnp.where(here, do, jnp.zeros_like(do))
            inner = jnp.sum(jnp.where(here, product, 0.0), axis=-1, keepdims=True)
            log = lse[:, half * HEAD : half * HEAD + 1]
            soft = jnp.exp(dot(q_here, keys, NT) + bias - log)
            grad = (soft * (dot(do_here, values, NT) - inner)).astype(BF16)
            outs.append(dot(grad, keys, NN))
            dk = dk + dot(q_here, grad, TN)
            dv = dv + dot(do_here, soft.astype(BF16), TN)
        dq_ref[at, :] = (jnp.where(low, outs[0], outs[1]) * SCALE).astype(BF16)
    dk, dv = dk.T, dv.T
    dk_ref[...] = dk[:rows]
    dkp_ref[...] = dk[rows:].astype(BF16)
    dv_ref[...] = dv[:rows]
    dvp_ref[...] = dv[rows:].astype(BF16)


def attend_back(qkv, kv_other, bias, out, lse, grad_out):
    rows, width = out.shape
    pairs = width // LANES
    spec = lambda base: pl.BlockSpec((rows, LANES), lambda p: (0, base + p))
    shape = lambda kind: jax.ShapeDtypeStruct((rows, width), kind)
    return pl.pallas_call(
        attend_back_kernel,
        out_shape=(shape(BF16), shape(F32), shape(F32), shape(BF16), shape(BF16)),
        grid=(pairs,),
        in_specs=[
            spec(0),
            spec(pairs),
            spec(2 * pairs),
            spec(0),
            spec(pairs),
            pl.BlockSpec((1, 2 * rows), lambda p: (0, 0)),
            spec(0),
            spec(0),
            spec(0),
        ],
        out_specs=(spec(0),) * 5,
        compiler_params=pltpu.CompilerParams(vmem_limit_bytes=56 << 20),
        name="attend_back",
    )(qkv, qkv, qkv, kv_other, kv_other, bias, out, lse, grad_out)


def gelu_parts(v):
    cdf = 0.5 * (1.0 + lax.erf(v * (2.0 ** -0.5)))
    pdf = jnp.exp(-0.5 * v * v) * 0.3989422804014327
    return v * cdf, cdf + v * pdf


def norm(values):
    center = values - jnp.mean(values, axis=-1, keepdims=True)
    inv_dev = lax.rsqrt(jnp.mean(center * center, axis=-1, keepdims=True) + EPS)
    return center * inv_dev, inv_dev


def norm_back(scaled, normed, inv_dev):
    return inv_dev * (
        scaled
        - jnp.mean(scaled, axis=-1, keepdims=True)
        - normed * jnp.mean(scaled * normed, axis=-1, keepdims=True)
    )


def on_device(
    frames_long,
    frames_short,
    length_long,
    length_short,
    input_proj,
    output_proj,
    expand_weight,
    shrink_weight,
    head_bias,
    expand_bias,
    row_params,
    cotangent_long,
    cotangent_short,
):
    mine = lax.axis_index("dp")
    depth = lax.axis_index("mp")
    n_dp = lax.axis_size("dp")
    core = mine % 2
    block = frames_short.shape[1]
    group = input_proj.shape[2]
    units = expand_weight.shape[1]
    width = group * N_MP
    shard = input_proj.shape[1]

    row_size, head_size = row_params.size, head_bias.size
    small = jnp.concatenate(
        [
            row_params.reshape(-1),
            head_bias.astype(F32).reshape(-1),
            expand_bias.astype(F32).reshape(-1),
            length_long.astype(F32),
            length_short.astype(F32),
        ]
    )
    pad = -small.size % LANES
    small = jnp.pad(small, (0, pad))[None]

    joined = jnp.concatenate(
        [input_proj[0], input_proj[1], input_proj[2], output_proj.T], axis=1
    )
    attn_parts = mp_gather(joined)
    order = [p[:, i * group : (i + 1) * group] for i in range(4) for p in attn_parts]
    attn_w = dp_gather(jnp.concatenate(order, axis=1))
    up_w = dp_gather(jnp.concatenate(mp_gather(expand_weight), axis=1))
    down_w = dp_gather(jnp.concatenate(mp_gather(shrink_weight.T), axis=1))

    everything = lax.all_gather(small, ("dp", "mp"), axis=0, tiled=True).reshape(
        n_dp, N_MP, -1
    )
    rows_of = everything[:, :, :row_size].reshape(n_dp, N_MP, 6, -1)
    row_vals = rows_of.transpose(2, 0, 1, 3).reshape(6, 1, width)
    relative = depth ^ jnp.arange(N_MP)
    at = row_size
    heads_of = everything[:, :, at : at + head_size].reshape(n_dp, N_MP, 2, -1)
    heads_of = heads_of.transpose(2, 1, 0, 3).reshape(2, N_MP, group)
    heads_of = jnp.take(heads_of, relative, axis=1).reshape(2, 1, width)
    at += head_size
    up_b = everything[:, :, at : at + expand_bias.size].transpose(1, 0, 2)
    up_b = jnp.take(up_b.reshape(N_MP, units), relative, axis=0).reshape(1, N_MP * units)
    at += expand_bias.size
    lengths = lax.dynamic_slice(everything, (mine - core, 0, at), (2, 1, 3))[:, 0]
    by_depth = jnp.stack([lengths[0, 0], lengths[1, 0], lengths[core, 1], lengths[core, 2]])
    length = by_depth[depth]

    is_long = depth < 2
    source = jnp.repeat(relative, block)
    inside = jnp.tile(jnp.arange(block), N_MP)
    stride = jnp.where(is_long, 2 * block, block)
    lead = jnp.where(is_long, block, 0)
    frame = (source * stride + inside).astype(F32)
    own_bias = jnp.where(frame + lead * core < length, 0.0, NEG_FILL)
    other_bias = jnp.where(
        is_long & (frame + lead * (1 - core) < length), 0.0, NEG_FILL
    )
    bias = jnp.concatenate([own_bias, other_bias])[None].astype(F32)

    x_low = to_clips(frames_long[0], frames_short, core, depth)
    cot = to_clips(cotangent_long[0], cotangent_short, core, depth)
    x = x_low.astype(F32)
    project = dot(x_low, attn_w[:, : 3 * width], NN)
    queries = ((project[:, :width] + heads_of[0]).astype(BF16) * SCALE).astype(BF16)
    kv = jnp.concatenate(
        [project[:, width : 2 * width], project[:, 2 * width :] + heads_of[1]], axis=1
    ).astype(BF16)
    qkv = jnp.concatenate([queries, kv], axis=1)
    kv_other = core_swap(kv)
    mixed, lse = attend(qkv, kv_other, bias)
    out_w = attn_w[:, 3 * width :]
    attention = dot(mixed, out_w, NT)
    n1, r1 = norm(x + attention + row_vals[0])
    h = n1 * row_vals[1] + row_vals[2]
    h_low = h.astype(BF16)
    act, slope = gelu_parts(dot(h_low, up_w, NN) + up_b)
    act = act.astype(BF16)
    n2, r2 = norm(h + dot(act, down_w, NT) + row_vals[3])
    result = (n2 * row_vals[4] + row_vals[5]).astype(BF16)
    result_long, result_short = from_clips(result, core, depth)

    gy = cot.astype(F32)
    dz = norm_back(gy * row_vals[4], n2, r2)
    df = dz.astype(BF16)
    du = (dot(df, down_w, NN) * slope).astype(BF16)
    g_down = dot(df, act, TN)
    g_up = dot(h_low, du, TN)
    dh = dz + dot(du, up_w, NT)
    da = norm_back(dh * row_vals[1], n1, r1)
    da_low = da.astype(BF16)
    do = dot(da_low, out_w, NN).astype(BF16)
    dq, dk, dv, dk_other, dv_other = attend_back(qkv, kv_other, bias, mixed, lse, do)
    back = core_swap(jnp.concatenate([dk_other, dv_other], axis=1)).astype(F32)
    dkv = (jnp.concatenate([dk, dv], axis=1) + back).astype(BF16)
    dqkv = jnp.concatenate([dq, dkv], axis=1)
    dx = dot(dqkv, attn_w[:, : 3 * width], NT)
    frames_grad = (da + dx).astype(BF16)
    grad_long, grad_short = from_clips(frames_grad, core, depth)

    g_attn = jnp.concatenate([dot(x_low, dqkv, TN), dot(da_low, mixed, TN)], axis=1)

    def halves(value):
        return [value[:, i * units : (i + 1) * units] for i in range(N_MP)]

    up_share = mp_scatter(halves(dp_scatter(g_up)))
    down_share = mp_scatter(halves(dp_scatter(g_down))).T
    attn_sum = dp_scatter(g_attn)
    attn_parts = [
        jnp.concatenate(
            [
                attn_sum[:, i * width + j * group : i * width + (j + 1) * group]
                for i in range(4)
            ],
            axis=1,
        )
        for j in range(N_MP)
    ]
    attn_share = mp_scatter(attn_parts)
    input_share = jnp.stack([attn_share[:, i * group : (i + 1) * group] for i in range(3)])
    output_share = attn_share[:, 3 * group :].T

    def total(value):
        return jnp.sum(value, axis=0)

    row_grads = jnp.stack(
        [total(da), total(dh * n1), total(dh), total(dz), total(gy * n2), total(gy)]
    )
    head_grads = jnp.stack([total(dq.astype(F32)), total(dkv[:, width:].astype(F32))])
    head_grads = jnp.take(head_grads.reshape(2, N_MP, group), relative, axis=1)
    up_b_grads = jnp.take(total(du.astype(F32)).reshape(N_MP, units), relative, axis=0)
    small_grads = jnp.concatenate(
        [
            row_grads.reshape(6, n_dp, N_MP, -1).transpose(1, 2, 0, 3).reshape(n_dp, N_MP, -1),
            head_grads.reshape(2, N_MP, n_dp, -1).transpose(2, 1, 0, 3).reshape(n_dp, N_MP, -1),
            up_b_grads.reshape(N_MP, n_dp, -1).transpose(1, 0, 2),
        ],
        axis=2,
    )
    small_share = lax.psum_scatter(
        jnp.pad(
            small_grads.reshape(n_dp * N_MP, -1),
            ((0, 0), (0, -small_grads.shape[2] % LANES)),
        ),
        ("dp", "mp"),
        scatter_dimension=0,
        tiled=True,
    )[0]
    return (
        result_long,
        result_short,
        grad_long.astype(F32),
        grad_short.astype(F32),
        input_share,
        output_share,
        up_share,
        down_share,
        small_share[row_size : row_size + head_size].reshape(2, 1, -1),
        small_share[row_size + head_size : row_size + head_size + expand_bias.size][None],
        small_share[:row_size].reshape(6, -1),
    )


def solution(mesh):
    return jax.shard_map(
        on_device,
        mesh=mesh,
        in_specs=(
            P("dp", "mp", None),
            P("dp", "mp", None),
            P("dp"),
            P("dp"),
            P(None, "dp", "mp"),
            P("mp", "dp"),
            P("dp", "mp"),
            P("mp", "dp"),
            P(None, "mp", "dp"),
            P("mp", "dp"),
            P(None, ("dp", "mp")),
            P("dp", "mp", None),
            P("dp", "mp", None),
        ),
        out_specs=(
            P("dp", "mp", None),
            P("dp", "mp", None),
            P("dp", "mp", None),
            P("dp", "mp", None),
            P(None, "dp", "mp"),
            P("mp", "dp"),
            P("dp", "mp"),
            P("mp", "dp"),
            P(None, "mp", "dp"),
            P("mp", "dp"),
            P(None, ("dp", "mp")),
        ),
        check_vma=False,
    )
```

time: 1220 us -> 947 us (0.78)
  waiting for transfers between devices: 750 us -> 98.2 us
  Pallas kernels: 0 us -> 468 us
  matrix products: 163 us -> 46.7 us
  starting transfers between devices: 2.37 us -> 73.1 us
  blocking collectives: 171 us -> 106 us
  local copies, waits for them, and re-layouts: 35.7 us -> 73.2 us
  between operations: 20.4 us -> 2.8 us
    pallas_call x0 -> x5, Pallas kernels: none -> 468 us  [the longest x3 434 us: place(): pl.pallas_call(functools.partial(place_kernel, len(pieces)), out_shape=ja...]
    reduce_scatter x15 -> x0, waiting for transfers between devices: 465 us -> none  [the longest x2 84.1 us: forward(): lax.psum_scatter(feed_parts[0].astype(jnp.bfloat16), 'mp', scatter_dimens...]
    all_gather x14 -> x0, waiting for transfers between devices: 279 us -> none  [the longest x2 76.5 us: forward(): lax.all_gather(h_low[0], 'mp', axis=1, tiled=True)]
    dot_general x35 -> x12, matrix products: 147 us -> 46.7 us  [dot(): return lax.dot_general(left, right, dims, preferred_element_type=F32)]
    ppermute x0 -> x54, waiting for transfers between devices: none -> 98.2 us  [the longest x24 51.7 us: dp_swap(): return lax.ppermute(value, 'dp', [(i, target(i)) for i in range(size)])]
    ppermute x0 -> x54, starting transfers between devices: none -> 73.1 us  [the longest x30 51.3 us: mp_swap(): return lax.ppermute(value, 'mp', [(i, i ^ step) for i in range(N_MP)])]
    all_gather x4 -> x1, blocking collectives: 103 us -> 65.7 us  [on_device(): lax.all_gather(small, ('dp', 'mp'), axis=0, tiled=True)]
    concatenate x3 -> x17, other arithmetic: 0.12 us -> 29.2 us  [the longest x1 8.81 us: on_device(): jnp.concatenate([dot(x_low, dqkv, TN), dot(da_low, mixed, TN)], axis=1)]
  transfers between devices with their start and end apart: 31 -> 54, of which waited for: 23 -> 14; matrix products, arithmetic and copies ran while one was open for 11% -> 15% of each run, Pallas kernels for 0% -> 48%
where the time goes in v1:
time: 947 us; the launch traced here: 939 us
  Pallas kernels  468 us (49%)
  blocking collectives  106 us (11%)
  waiting for transfers between devices  98.2 us (10%)
  local copies, waits for them, and re-layouts  73.2 us (8%)
  starting transfers between devices  73.1 us (8%)
  other arithmetic  71.1 us (8%)
  matrix products  46.7 us (5%)
    pallas_call x3, Pallas kernels, place(): pl.pallas_call(functools.partial(place_kernel, len(pieces)), out_shape=ja...  434 us
    all_gather x1, blocking collectives, on_device(): lax.all_gather(small, ('dp', 'mp'), axis=0, tiled=True)  65.7 us
    ppermute x24, waiting for transfers between devices, dp_swap(): return lax.ppermute(value, 'dp', [(i, target(i)) for i in range(size)])  51.7 us
    ppermute x30, starting transfers between devices, mp_swap(): return lax.ppermute(value, 'mp', [(i, i ^ step) for i in range(N_MP)])  51.3 us
    dot_general x12, matrix products, dot(): return lax.dot_general(left, right, dims, preferred_element_type=F32)  46.7 us
    ppermute x30, waiting for transfers between devices, mp_swap(): return lax.ppermute(value, 'mp', [(i, i ^ step) for i in range(N_MP)])  46.4 us
    unnamed x1, blocking collectives  40.1 us
    ppermute x24, starting transfers between devices, dp_swap(): return lax.ppermute(value, 'dp', [(i, target(i)) for i in range(size)])  21.8 us
  transfers between devices with their start and end apart: 54, of which 14 were waited for; matrix products, arithmetic and copies ran while one was open for 15% of the time, Pallas kernels for 48%

profile of v1, /device:TPU:0, one launch (start us, length us, event | category | flops | bytes accessed | tf_op | source)
XLA Modules:
  0.0 938.6 jit_solution(3712057231629133541)
XLA Ops:
  2.6 5.1 collective-permute-start.6
  16.4 10.3 %collective-permute-done.5 = bf16[96,768]{1,0:T(8,128)(2,1)S(1)} collective-permute-done((bf16[96,768]{1,0:T(8,128)(2,1)S(1)}, bf16[96,768]{1,0:T(8,128)(2,1)S(1)}, u32[]{:S(2)}, u32[]{:S(2)}) %collective-permute-start.5) | collective-permute-done | bytes 147488 | tf_op jit(solution)/shard_map/ppermute | solution.py:29
  29.7 65.7 %all-gather.1 = f32[32,1,384]{2,1,0:T(1,128)S(1)} all-gather(f32[1,1,384]{2,1,0:T(1,128)S(1)} %reshape.328), channel_id=2, replica_groups=mesh['dp'=8,'mp'=4] {'dp','mp'}, dimensions={0}, use_global_device_ids=true | all-gather | bytes 50688 | tf_op jit(solution)/shard_map/all_gather | solution.py:342
  104.3 5.5 collective-permute-done.18
  112.9 8.0 collective-permute-done.8.refs_2_
  140.2 5.5 collective-permute-start.2
  148.7 5.8 collective-permute-done.21.refs_2_
  156.7 144.8 %place.3 = bf16[8,96,3072]{2,1,0:T(8,128)(2,1)} custom-call(s32[8]{0:T(128)} %stack.206.table, bf16[1,96,3072]{2,1,0:T(8,128)(2,1)} %bitcast.182, bf16[1,96,3072]{2,1,0:T(8,128)(2,1)} %copy-done.4, bf16[2,96,3072]{2,1,0:T(8,128)(2,1)} %collective-permute-done.8.refs_2_, bf16[4,96,3072]{2,1,0:T(8,128)(2,1)} %collective-permute-done.9.refs_3_), custom_call_target="tpu_custom_call" | custom-call | tf_op jit(solution)/shard_map/place/pallas_call | solution.py:104
  334.6 144.8 %place.4 = bf16[8,96,3072]{2,1,0:T(8,128)(2,1)} custom-call(s32[8]{0:T(128)} %stack.206.table, bf16[1,96,3072]{2,1,0:T(8,128)(2,1)} %copy-done.1, bf16[1,96,3072]{2,1,0:T(8,128)(2,1)} %copy-done.5, bf16[2,96,3072]{2,1,0:T(8,128)(2,1)} %collective-permute-done.15.refs_2_, bf16[4,96,3072]{2,1,0:T(8,128)(2,1)} %collective-permute-done.16.refs_3_), custom_call_target="tpu_custom_call" | custom-call | tf_op jit(solution)/shard_map/place/pallas_call | solution.py:104
  479.4 144.8 %place.5 = bf16[8,96,3072]{2,1,0:T(8,128)(2,1)} custom-call(s32[8]{0:T(128)} %stack.206.table, bf16[1,96,3072]{2,1,0:T(8,128)(2,1)} %copy-done.2, bf16[1,96,3072]{2,1,0:T(8,128)(2,1)} %copy-done.6, bf16[2,96,3072]{2,1,0:T(8,128)(2,1)} %copy-done.18, bf16[4,96,3072]{2,1,0:T(8,128)(2,1)} %collective-permute-done.22.refs_3_), custom_call_target="tpu_custom_call" | custom-call | tf_op jit(solution)/shard_map/place/pallas_call | solution.py:104
  628.1 15.1 %attend.1 = (bf16[512,768]{1,0:T(8,128)(2,1)}, f32[512,768]{1,0:T(8,128)}) custom-call(bf16[512,2304]{1,0:T(8,128)(2,1)} %pad_maximum_fusion.2.q_ref.k_ref.v_ref, bf16[512,2304]{1,0:T(8,128)(2,1)} %pad_maximum_fusion.2.q_ref.k_ref.v_ref, bf16[512,2304]{1,0:T(8,128)(2,1)} %pad_maximum_fusion.2.q_ref.k_ref.v_ref, bf16[512,1536]{1,0:T(8,128)(2,1)} %copy-done, ...), custom_call_target="tpu_custom_call" | custom-call | tf_op jit(solution)/shard_map/attend/pallas_call | solution.py:191
  646.7 6.1 multiply_convert_fusion
  663.5 7.4 convert_reduce_fusion
  699.9 18.4 %attend_back.1 = (bf16[512,768]{1,0:T(8,128)(2,1)}, f32[512,768]{1,0:T(8,128)}, f32[512,768]{1,0:T(8,128)}, bf16[512,768]{1,0:T(8,128)(2,1)}, bf16[512,768]{1,0:T(8,128)(2,1)}) custom-call(bf16[512,2304]{1,0:T(8,128)(2,1)} %pad_maximum_fusion.2.q_ref.k_ref.v_ref, bf16[512,2304]{1,0:T(8,128)(2,1)} %pad_maximum_fusion.2.q_ref.k_ref.v_ref, ...), custom_call_target="tpu_custom_call" | custom-call | tf_op jit(solution)/shard_map/attend_back/pallas_call | solution.py:254
  739.2 8.6 collective-permute-done.24
  766.2 6.0 fusion.20
  772.2 8.8 pad_maximum_fusion
  794.1 40.1 %all-reduce.2 = f32[32,384]{1,0:T(8,128)} all-reduce(f32[32,384]{1,0:T(8,128)} %select_maximum_fusion), channel_id=3, replica_groups=mesh['dp'=8,'mp'=4] {'dp','mp'}, use_global_device_ids=true, to_apply=%region_17.20.clone | all-reduce | flops 12288 | bytes 98304
  851.4 9.3 collective-permute-done.49
  863.2 16.5 %collective-permute-done.43 = bf16[2,96,3072]{2,1,0:T(8,128)(2,1)S(1)} collective-permute-done((bf16[2,96,3072]{2,1,0:T(8,128)(2,1)S(1)}, bf16[2,96,3072]{2,1,0:T(8,128)(2,1)S(1)}, u32[]{:S(2)}, u32[]{:S(2)}) %collective-permute-start.43) | collective-permute-done | bytes 1179680 | tf_op jit(solution)/shard_map/ppermute | solution.py:34
  889.8 4.5 collective-permute-done.44
  894.5 7.6 collective-permute-done.37
  912.6 6.6 collective-permute-done.46
  927.7 8.9 collective-permute-done.40
  (404 shorter events, 231.8 us)
Async XLA Ops:
  8.3 92.4 %collective-permute-start.11 = (bf16[96,768]{1,0:T(8,128)(2,1)}, bf16[96,768]{1,0:T(8,128)(2,1)S(1)}, u32[]{:S(2)}, u32[]{:S(2)}) collective-permute-start(bf16[96,768]{1,0:T(8,128)(2,1)} %param.23), channel_id=1, source_target_pairs={{0,1},{1,0},{2,3},{3,2},{4,5},{5,4},{6,7},{7,6},{8,9},{9,8},{10,11... | collective-permute-start | bytes 442376 | tf_op jit(solution)/shard_map/ppermute | solution.py:29
  9.7 91.1 %collective-permute-start.12 = (bf16[96,768]{1,0:T(8,128)(2,1)}, bf16[96,768]{1,0:T(8,128)(2,1)S(1)}, u32[]{:S(2)}, u32[]{:S(2)}) collective-permute-start(bf16[96,768]{1,0:T(8,128)(2,1)} %param.23), channel_id=1, source_target_pairs={{0,2},{1,3},{2,0},{3,1},{4,6},{5,7},{6,4},{7,5},{8,10},{9,11},{10,... | collective-permute-start | bytes 442376 | tf_op jit(solution)/shard_map/ppermute | solution.py:29
  12.6 90.9 %collective-permute-start.13 = (bf16[96,768]{1,0:T(8,128)(2,1)}, bf16[96,768]{1,0:T(8,128)(2,1)S(1)}, u32[]{:S(2)}, u32[]{:S(2)}) collective-permute-start(bf16[96,768]{1,0:T(8,128)(2,1)} %param.23), channel_id=1, source_target_pairs={{0,3},{1,2},{2,1},{3,0},{4,7},{5,6},{6,5},{7,4},{8,11},{9,10},{10,... | collective-permute-start | bytes 442376 | tf_op jit(solution)/shard_map/ppermute | solution.py:29
  26.7 76.9 %collective-permute-start.17 = (bf16[96,768]{1,0:T(8,128)(2,1)}, bf16[96,768]{1,0:T(8,128)(2,1)S(1)}, u32[]{:S(2)}, u32[]{:S(2)}) collective-permute-start(bf16[96,768]{1,0:T(8,128)(2,1)} %bitcast.206), channel_id=1, source_target_pairs={{0,1},{1,0},{2,3},{3,2},{4,5},{5,4},{6,7},{7,6},{8,9},{9,8},{10,11... | collective-permute-start | bytes 442376 | tf_op jit(solution)/shard_map/ppermute | solution.py:29
  27.4 69.1 %collective-permute-start.7 = (bf16[1,96,3072]{2,1,0:T(8,128)(2,1)S(1)}, bf16[1,96,3072]{2,1,0:T(8,128)(2,1)S(1)}, u32[]{:S(2)}, u32[]{:S(2)}) collective-permute-start(bf16[1,96,3072]{2,1,0:T(8,128)(2,1)S(1)} %bitcast.179), channel_id=1, source_target_pairs={{0,8},{4,20},{8,0},{12,28},{16,24},{20,4},{24,16},{28,12},{1,9},{5... | collective-permute-start | bytes 1769480 | tf_op jit(solution)/shard_map/ppermute | solution.py:34
  103.5 33.4 %collective-permute-start = (bf16[128,768]{1,0:T(8,128)(2,1)S(1)}, bf16[128,768]{1,0:T(8,128)(2,1)}, u32[]{:S(2)}, u32[]{:S(2)}) collective-permute-start(bf16[128,768]{1,0:T(8,128)(2,1)S(1)} %dynamic-slice_bitcast_fusion.9), channel_id=1, source_target_pairs={{0,4},{4,0},{8,12},{12,8},{16,20},{20,16},{24,28},{28,24},{1,5},{5... | collective-permute-start | bytes 589832 | tf_op jit(solution)/shard_map/ppermute | solution.py:34
  103.6 33.3 %collective-permute-start.27 = (bf16[128,768]{1,0:T(8,128)(2,1)S(1)}, bf16[128,768]{1,0:T(8,128)(2,1)}, u32[]{:S(2)}, u32[]{:S(2)}) collective-permute-start(bf16[128,768]{1,0:T(8,128)(2,1)S(1)} %dynamic-slice_bitcast_fusion.4), channel_id=1, source_target_pairs={{0,4},{4,0},{8,12},{12,8},{16,20},{20,16},{24,28},{28,24},{1,5},{5... | collective-permute-start | bytes 589832 | tf_op jit(solution)/shard_map/ppermute | solution.py:34
  123.8 32.5 %collective-permute-start.9 = (bf16[4,96,3072]{2,1,0:T(8,128)(2,1)}, bf16[4,96,3072]{2,1,0:T(8,128)(2,1)}, u32[]{:S(2)}, u32[]{:S(2)}) collective-permute-start(bf16[4,96,3072]{2,1,0:T(8,128)(2,1)} %pad_maximum_fusion.1), channel_id=1, source_target_pairs={{0,4},{4,0},{8,12},{12,8},{16,20},{20,16},{24,28},{28,24},{1,5},{5... | collective-permute-start | bytes 7077896 | tf_op jit(solution)/shard_map/ppermute | solution.py:34
  140.2 161.3 %collective-permute-start.1 = (bf16[128,768]{1,0:T(8,128)(2,1)}, bf16[128,768]{1,0:T(8,128)(2,1)}, u32[]{:S(2)}, u32[]{:S(2)}) collective-permute-start(bf16[128,768]{1,0:T(8,128)(2,1)} %get-tuple-element.136), channel_id=1, source_target_pairs={{0,1},{1,0},{2,3},{3,2},{4,5},{5,4},{6,7},{7,6},{8,9},{9,8},{10,11... | collective-permute-start | bytes 589832 | tf_op jit(solution)/shard_map/ppermute | solution.py:29
  140.2 161.3 %collective-permute-start.2 = (bf16[128,768]{1,0:T(8,128)(2,1)}, bf16[128,768]{1,0:T(8,128)(2,1)}, u32[]{:S(2)}, u32[]{:S(2)}) collective-permute-start(bf16[128,768]{1,0:T(8,128)(2,1)} %get-tuple-element.135), channel_id=1, source_target_pairs={{0,2},{1,3},{2,0},{3,1},{4,6},{5,7},{6,4},{7,5},{8,10},{9,11},{10,... | collective-permute-start | bytes 589832 | tf_op jit(solution)/shard_map/ppermute | solution.py:29
  145.7 155.8 %collective-permute-start.3 = (bf16[128,768]{1,0:T(8,128)(2,1)}, bf16[128,768]{1,0:T(8,128)(2,1)}, u32[]{:S(2)}, u32[]{:S(2)}) collective-permute-start(bf16[128,768]{1,0:T(8,128)(2,1)} %get-tuple-element.134), channel_id=1, source_target_pairs={{0,3},{1,2},{2,1},{3,0},{4,7},{5,6},{6,5},{7,4},{8,11},{9,10},{10,... | collective-permute-start | bytes 589832 | tf_op jit(solution)/shard_map/ppermute | solution.py:29
  154.6 175.6 %collective-permute-start.16 = (bf16[4,96,3072]{2,1,0:T(8,128)(2,1)}, bf16[4,96,3072]{2,1,0:T(8,128)(2,1)}, u32[]{:S(2)}, u32[]{:S(2)}) collective-permute-start(bf16[4,96,3072]{2,1,0:T(8,128)(2,1)} %pad_maximum_fusion.3), channel_id=1, source_target_pairs={{0,4},{4,0},{8,12},{12,8},{16,20},{20,16},{24,28},{28,24},{1,5},{5... | collective-permute-start | bytes 7077896 | tf_op jit(solution)/shard_map/ppermute | solution.py:34
  156.3 323.1 %collective-permute-start.22 = (bf16[4,96,3072]{2,1,0:T(8,128)(2,1)}, bf16[4,96,3072]{2,1,0:T(8,128)(2,1)}, u32[]{:S(2)}, u32[]{:S(2)}) collective-permute-start(bf16[4,96,3072]{2,1,0:T(8,128)(2,1)} %pad_maximum_fusion.4), channel_id=1, source_target_pairs={{0,4},{4,0},{8,12},{12,8},{16,20},{20,16},{24,28},{28,24},{1,5},{5... | collective-permute-start | bytes 7077896 | tf_op jit(solution)/shard_map/ppermute | solution.py:34
  308.9 318.0 %collective-permute-start.10 = (bf16[512,1536]{1,0:T(8,128)(2,1)}, bf16[512,1536]{1,0:T(8,128)(2,1)S(1)}, u32[]{:S(2)}, u32[]{:S(2)}) collective-permute-start(bf16[512,1536]{1,0:T(8,128)(2,1)} %pad_maximum_fusion.9), channel_id=1, source_target_pairs={{0,4},{4,0},{8,12},{12,8},{16,20},{20,16},{24,28},{28,24},{1,5},{5... | collective-permute-start | bytes 4718600 | tf_op jit(solution)/shard_map/ppermute | solution.py:34
  330.2 325.8 %collective-permute-start.28 = (bf16[128,768]{1,0:T(8,128)(2,1)}, bf16[128,768]{1,0:T(8,128)(2,1)S(1)}, u32[]{:S(2)}, u32[]{:S(2)}) collective-permute-start(bf16[128,768]{1,0:T(8,128)(2,1)} %get-tuple-element.125), channel_id=1, source_target_pairs={{0,1},{1,0},{2,3},{3,2},{4,5},{5,4},{6,7},{7,6},{8,9},{9,8},{10,11... | collective-permute-start | bytes 589832 | tf_op jit(solution)/shard_map/ppermute | solution.py:29
  330.2 325.8 %collective-permute-start.29 = (bf16[128,768]{1,0:T(8,128)(2,1)}, bf16[128,768]{1,0:T(8,128)(2,1)}, u32[]{:S(2)}, u32[]{:S(2)}) collective-permute-start(bf16[128,768]{1,0:T(8,128)(2,1)} %get-tuple-element.124), channel_id=1, source_target_pairs={{0,2},{1,3},{2,0},{3,1},{4,6},{5,7},{6,4},{7,5},{8,10},{9,11},{10,... | collective-permute-start | bytes 589832 | tf_op jit(solution)/shard_map/ppermute | solution.py:29
  330.2 325.8 %collective-permute-start.30 = (bf16[128,768]{1,0:T(8,128)(2,1)}, bf16[128,768]{1,0:T(8,128)(2,1)}, u32[]{:S(2)}, u32[]{:S(2)}) collective-permute-start(bf16[128,768]{1,0:T(8,128)(2,1)} %get-tuple-element.123), channel_id=1, source_target_pairs={{0,3},{1,2},{2,1},{3,0},{4,7},{5,6},{6,5},{7,4},{8,11},{9,10},{10,... | collective-permute-start | bytes 589832 | tf_op jit(solution)/shard_map/ppermute | solution.py:29
  721.0 30.9 %collective-permute-start.31 = (bf16[512,1536]{1,0:T(8,128)(2,1)}, bf16[512,1536]{1,0:T(8,128)(2,1)}, u32[]{:S(2)}, u32[]{:S(2)}) collective-permute-start(bf16[512,1536]{1,0:T(8,128)(2,1)} %pad_maximum_fusion.10), channel_id=1, source_target_pairs={{0,4},{4,0},{8,12},{12,8},{16,20},{20,16},{24,28},{28,24},{1,5},{5... | collective-permute-start | bytes 4718600 | tf_op jit(solution)/shard_map/ppermute | solution.py:34
  729.9 111.4 %collective-permute-start.48 = (bf16[4,96,3072]{2,1,0:T(8,128)(2,1)}, bf16[4,96,3072]{2,1,0:T(8,128)(2,1)}, u32[]{:S(2)}, u32[]{:S(2)}) collective-permute-start(bf16[4,96,3072]{2,1,0:T(8,128)(2,1)} %pad_maximum_fusion.8), channel_id=1, source_target_pairs={{0,4},{4,0},{8,12},{12,8},{16,20},{20,16},{24,28},{28,24},{1,5},{5... | collective-permute-start | bytes 7077896 | tf_op jit(solution)/shard_map/ppermute | solution.py:34
  749.8 97.7 %collective-permute-start.42 = (bf16[4,96,3072]{2,1,0:T(8,128)(2,1)}, bf16[4,96,3072]{2,1,0:T(8,128)(2,1)}, u32[]{:S(2)}, u32[]{:S(2)}) collective-permute-start(bf16[4,96,3072]{2,1,0:T(8,128)(2,1)} %pad_maximum_fusion.7), channel_id=1, source_target_pairs={{0,4},{4,0},{8,12},{12,8},{16,20},{20,16},{24,28},{28,24},{1,5},{5... | collective-permute-start | bytes 7077896 | tf_op jit(solution)/shard_map/ppermute | solution.py:34
  760.0 78.3 %collective-permute-start.32 = (bf16[128,768]{1,0:T(8,128)(2,1)}, bf16[128,768]{1,0:T(8,128)(2,1)}, u32[]{:S(2)}, u32[]{:S(2)}) collective-permute-start(bf16[128,768]{1,0:T(8,128)(2,1)} %get-tuple-element.121), channel_id=1, source_target_pairs={{0,1},{1,0},{2,3},{3,2},{4,5},{5,4},{6,7},{7,6},{8,9},{9,8},{10,11... | collective-permute-start | bytes 589832 | tf_op jit(solution)/shard_map/ppermute | solution.py:29
  763.8 74.5 %collective-permute-start.33 = (bf16[128,768]{1,0:T(8,128)(2,1)}, bf16[128,768]{1,0:T(8,128)(2,1)}, u32[]{:S(2)}, u32[]{:S(2)}) collective-permute-start(bf16[128,768]{1,0:T(8,128)(2,1)} %get-tuple-element.120), channel_id=1, source_target_pairs={{0,2},{1,3},{2,0},{3,1},{4,6},{5,7},{6,4},{7,5},{8,10},{9,11},{10,... | collective-permute-start | bytes 589832 | tf_op jit(solution)/shard_map/ppermute | solution.py:29
  763.8 74.5 %collective-permute-start.34 = (bf16[128,768]{1,0:T(8,128)(2,1)}, bf16[128,768]{1,0:T(8,128)(2,1)}, u32[]{:S(2)}, u32[]{:S(2)}) collective-permute-start(bf16[128,768]{1,0:T(8,128)(2,1)} %get-tuple-element.119), channel_id=1, source_target_pairs={{0,3},{1,2},{2,1},{3,0},{4,7},{5,6},{6,5},{7,4},{8,11},{9,10},{10,... | collective-permute-start | bytes 589832 | tf_op jit(solution)/shard_map/ppermute | solution.py:29
  838.3 43.9 %collective-permute-start.36 = (bf16[4,96,3072]{2,1,0:T(8,128)(2,1)}, bf16[4,96,3072]{2,1,0:T(8,128)(2,1)S(1)}, u32[]{:S(2)}, u32[]{:S(2)}) collective-permute-start(bf16[4,96,3072]{2,1,0:T(8,128)(2,1)} %pad_maximum_fusion.6), channel_id=1, source_target_pairs={{0,4},{4,0},{8,12},{12,8},{16,20},{20,16},{24,28},{28,24},{1,5},{5... | collective-permute-start | bytes 7077896 | tf_op jit(solution)/shard_map/ppermute | solution.py:34
  (92 other events, 1347.6 us)
